TPU v7x, 512 devices: a whole 4x8x8 slice. The times are simulated.
512 devices in a mesh: feat: 128 (over x, y, z_hi), rows: 4 (over z_lo, core).
Axes of the slice: x: 4, y: 8, z: 8 (z_hi: 4, z_lo: 2; z = z_hi * 2 + z_lo), core: 2. Of those that a mesh axis runs over, the one named last changes fastest.
Arguments:
- binned: int32 [8192, 8192], P('rows', 'feat'), may hold values from 0 to 255
- node_of: int32 [8192], P('rows'), may hold values from 0 to 31
- margin: float32 [8192], P('rows'), may hold values from -6 to 6
- labels: float32 [8192], P('rows'), may hold values from 0 to 1
- split_feature: int32 [32], replicated, may hold values from 0 to 8191
- split_bin: int32 [32], replicated, may hold values from 0 to 255
Outputs:
- histogram: float32 [32, 2, 8192, 256], P('rows', None, 'feat')
- margin_out: float32 [8192], P('rows')
- child_out: int32 [8192], P('rows')
- grad_out: float32 [2, 8192], P(None, 'rows')
All inputs are finite; a program needn't handle non-finite values.
Results may differ from a plain program's by a relative error of at most 0.0045.
Values may be sent and summed in bfloat16 or wider, within the bound.
No kernel may reach another device: no remote copies, remote signals or barrier semaphores. Data moves between devices by JAX's collectives and lax.ppermute only.
A program may use at most 64 MiB of HBM per device.

v0:
```python
import functools

import jax
import jax.numpy as jnp
from jax import lax
from jax.experimental import pallas as pl
from jax.experimental.pallas import tpu as pltpu
from jax.sharding import Mesh
from jax.sharding import PartitionSpec as P

BINS = 256
NODES = 32
ROWS = 2048
FEATS = 64
TILE = 256
CUT = 48
FEAT_AXES = ("x", "y", "zh")
ROW_AXES = ("zl", "core")
PLANE = ("x", "y")
LINE = ("zh", "zl", "core")
F32 = jnp.float32
BF16 = jnp.bfloat16
I16 = jnp.int16
LIMIT = pltpu.CompilerParams(vmem_limit_bytes=16 << 20)
VMEM = pl.BlockSpec(memory_space=pltpu.VMEM)


def near(array):
    return pltpu.with_memory_space_constraint(array, pltpu.VMEM)


def far(array):
    return pltpu.with_memory_space_constraint(array, pltpu.HBM)


def iota(shape, dim):
    return lax.broadcasted_iota(jnp.int32, shape, dim)


def cost(flops, moved):
    return pl.CostEstimate(flops=flops, bytes_accessed=moved, transcendentals=0)


def contract_last(a, b):
    return lax.dot_general(a, b, (((1,), (1,)), ((), ())), preferred_element_type=F32)


def bin_sums(weights, row_of):
    low_ids = iota((BINS // 2, TILE), 0).astype(I16)
    one, zero = BF16(1), BF16(0)
    total = None
    for k in range(ROWS // TILE):
        row = jnp.broadcast_to(row_of(k), (16, TILE))
        low = jnp.concatenate([(row & 127).astype(I16)] * 8, axis=0)
        high = jnp.concatenate([(row >> 7).astype(I16)] * 4, axis=0)
        tile = weights[:, k * TILE : (k + 1) * TILE]
        split = [jnp.where(high == h, tile, zero) for h in range(2)]
        hot = jnp.where(low_ids == low, one, zero)
        piece = contract_last(jnp.concatenate(split, axis=0), hot)
        total = piece if total is None else total + piece
    return total


def pair_sums(weights, row_of, row_of_next):
    low_ids = iota((BINS // 2, TILE), 0).astype(I16)
    one, zero = BF16(1), BF16(0)
    total = None
    for k in range(ROWS // TILE):
        tile = weights[:, k * TILE : (k + 1) * TILE]
        parts, hots = [tile], []
        for source in (row_of, row_of_next):
            row = jnp.broadcast_to(source(k), (16, TILE))
            low = jnp.concatenate([(row & 127).astype(I16)] * 8, axis=0)
            high = jnp.concatenate([(row >> 7).astype(I16)] * 4, axis=0)
            parts.append(jnp.where(high == 1, tile, zero))
            hots.append(jnp.where(low_ids == low, one, zero))
        piece = contract_last(jnp.concatenate(parts, axis=0), jnp.concatenate(hots, axis=0))
        total = piece if total is None else total + piece
    sums = []
    for i in range(2):
        span = slice(i * 128, (i + 1) * 128)
        upper = total[64 * (i + 1) : 64 * (i + 2), span]
        sums.append((total[:64, span] - upper, upper))
    return sums


def stage_kernel(columns, node, margin, labels, feature, cut, weights, pay, chosen):
    here = lax.axis_index("zl") * 2 + lax.axis_index("core")
    feat_start = (
        (lax.axis_index("x") * 8 + lax.axis_index("y")) * 4 + lax.axis_index("zh")
    ) * FEATS
    probability = jax.nn.sigmoid(margin[...])
    gradient = probability - labels[...]
    hessian = probability * (1.0 - probability)
    q = iota((2 * NODES, 1), 0)
    block = q // 16
    block = jnp.where(block < 2, 2 * block + 1, 2 * block - 4)
    node_q = (block * 8 + (q % 16) // 2) ^ (here * 8)
    channel = q % 2
    values = jnp.where(channel == 0, gradient, hessian)
    weights[...] = jnp.where(node[...] == node_q, values, 0.0).astype(BF16)
    local = feature[...] - feat_start
    diagonal = iota((NODES, NODES), 0) == iota((NODES, NODES), 1)
    local_n = jnp.sum(jnp.where(diagonal, local, 0), axis=1, keepdims=True)
    cut_n = jnp.sum(jnp.where(diagonal, cut[...], 0), axis=1, keepdims=True)
    owned_n = (local_n >= 0) & (local_n < FEATS)
    chooser = jnp.where(iota((NODES, FEATS), 1) == local_n, 1.0, 0.0).astype(BF16)
    split_values = jnp.dot(
        chooser, columns[...].astype(F32).astype(BF16), preferred_element_type=F32
    )
    hot = node[...] == iota((NODES, ROWS), 0)
    value = jnp.sum(jnp.where(hot, split_values, 0.0), axis=0, keepdims=True)
    owned = jnp.sum(jnp.where(hot & owned_n, 1.0, 0.0), axis=0, keepdims=True)
    row_cut = jnp.sum(jnp.where(hot, cut_n.astype(F32), 0.0), axis=0, keepdims=True)
    right = jnp.where(value > row_cut, owned, 0.0)
    chosen[...] = jnp.where(owned > 0.5, value, -1.0).astype(jnp.int32)
    sums = bin_sums(weights, lambda k: chosen[:, k * TILE : (k + 1) * TILE])
    sums = jnp.concatenate([sums[:64], sums[64:]], axis=1).astype(BF16).astype(F32)
    cut_q = jnp.sum(
        jnp.where(iota((2 * NODES, NODES), 1) == node_q, cut[...], 0), axis=1, keepdims=True
    )
    below = iota((2 * NODES, BINS), 1) <= cut_q
    left = jnp.sum(jnp.where(below, sums, 0.0), axis=1, keepdims=True)
    whole = jnp.sum(sums, axis=1, keepdims=True)
    lane = iota((2 * NODES, 128), 1)
    slot = 2 * node_q + channel
    entries = jnp.where(lane == slot, left, 0.0) + jnp.where(lane == slot + 64, whole, 0.0)
    half = ROWS // 2
    lines = [
        right[:, i * 128 : (i + 1) * 128] + 2.0 * right[:, half + i * 128 : half + (i + 1) * 128]
        for i in range(8)
    ]
    lines.append(jnp.sum(entries, axis=0, keepdims=True))
    for p in range(16):
        for i in range(9):
            pay[p, i] = lines[i]


def stage(columns, node, margin, labels, feature, cut):
    return pl.pallas_call(
        stage_kernel,
        out_shape=(
            pltpu.VMEM((2 * NODES, ROWS), BF16),
            pltpu.VMEM((16, 9, 1, 128), F32),
        ),
        in_specs=[VMEM] * 6,
        out_specs=[VMEM] * 2,
        scratch_shapes=[pltpu.VMEM((1, ROWS), jnp.int32)],
        name="stage",
        compiler_params=LIMIT,
        cost_estimate=cost(2 * 96 * ROWS * FEATS, 3 << 20),
    )(columns, node, margin, labels, feature, cut)


def histogram_kernel(first, count, weights, columns, send, keep):
    def pair(p, carry):
        f = 2 * p

        def source(g):
            return lambda k: columns[pl.ds(first + g, 1), k * TILE : (k + 1) * TILE]

        for i, halves in enumerate(pair_sums(weights, source(f), source(f + 1))):
            for h in range(2):
                span = slice(h * 128, (h + 1) * 128)
                sums = halves[h].astype(BF16)
                send[f + i, :, span] = sums[:NODES]
                keep[f + i, :, span] = sums[NODES:]
        return carry

    lax.fori_loop(0, count // 2, pair, 0, unroll=4)


def histograms(weights, columns, first, count):
    half = pltpu.VMEM((count, NODES, BINS), BF16)
    return pl.pallas_call(
        functools.partial(histogram_kernel, first, count),
        out_shape=(half, half),
        in_specs=[VMEM] * 2,
        out_specs=[VMEM] * 2,
        compiler_params=LIMIT,
        cost_estimate=cost(2 * 64 * ROWS * count * BINS, 3 << 20),
    )(weights, columns)


def chip_sum_kernel(keep, arrived, sent, own, send):
    for f in range(0, keep.shape[0], 8):
        total = keep[f : f + 8].astype(F32) + arrived[f : f + 8].astype(F32)
        own[f : f + 8] = total[:, :16]
        send[f : f + 8] = total[:, 16:].astype(BF16)


def chip_sum(keep, arrived, sent):
    count = keep.shape[0]
    return pl.pallas_call(
        chip_sum_kernel,
        out_shape=(
            pltpu.VMEM((count, 16, BINS), F32),
            pltpu.VMEM((count, 16, BINS), BF16),
        ),
        in_specs=[VMEM, VMEM, pl.BlockSpec(memory_space=pl.ANY)],
        out_specs=[VMEM] * 2,
        name="chip_sum",
        compiler_params=LIMIT,
        cost_estimate=cost(count * 32 * BINS, 3 << 20),
    )(near(keep), near(arrived), near(sent))


def relay_kernel(line, sent, pay):
    here = lax.axis_index("zl") * 2 + lax.axis_index("core")
    for i in range(9):
        total = line[here, i] if i < 8 else line[0, i]
        for m in range(1, 4 if i < 8 else 16):
            total = total + (line[4 * m + here, i] if i < 8 else line[m, i])
        for p in range(32):
            pay[p, i] = total


def relay(line, sent):
    return pl.pallas_call(
        relay_kernel,
        out_shape=pltpu.VMEM((32, 9, 1, 128), F32),
        in_specs=[VMEM, pl.BlockSpec(memory_space=pl.ANY)],
        out_specs=VMEM,
        name="relay",
        compiler_params=LIMIT,
        cost_estimate=cost(32 * 9 * 128, 1 << 17),
    )(near(line), near(sent))


def finish_kernel(count, own, arrived, sent, *rest):
    histogram, total = rest[-2:]
    for f in range(0, count, 8):
        piece = (own[f : f + 8] + arrived[f : f + 8].astype(F32)).reshape(128, BINS)
        for h in range(2):
            total[h, f * 16 : (f + 8) * 16, :] = piece[:, h * 128 : (h + 1) * 128]
    for q in range(16):
        for h in range(2):
            histogram[q, :, h * 128 : (h + 1) * 128] = total[h, pl.ds(q, count, stride=16), :]


def finish(own, arrived, sent, first, so_far=None):
    count = own.shape[0]
    anywhere = pl.BlockSpec(memory_space=pl.ANY)
    more = () if so_far is None else (so_far,)
    return pl.pallas_call(
        functools.partial(finish_kernel, count),
        out_shape=jax.ShapeDtypeStruct((16, FEATS, BINS), F32),
        grid=(1,),
        in_specs=[VMEM, VMEM, anywhere] + [anywhere] * len(more),
        out_specs=pl.BlockSpec((16, count, BINS), lambda i: (0, first // count, 0)),
        scratch_shapes=[pltpu.VMEM((2, count * 16, 128), F32)],
        input_output_aliases={3: 0} if more else {},
        compiler_params=LIMIT,
        cost_estimate=cost(count * 16 * BINS, 3 << 20),
    )(near(own), near(arrived), near(sent), *more)


def rows_kernel(parts, node, margin, labels, sent, margin_out, child_out, grad_out, codes_ref):
    for i in range(8):
        line = parts[0, i]
        for p in range(1, 32):
            line = line + parts[p, i]
        codes_ref[i : i + 1, :] = line
    table = parts[0, 8]
    for p in range(1, 32):
        table = table + parts[p, 8]
    codes = codes_ref[...]
    table = jnp.broadcast_to(table, (8, 128))
    rest = pltpu.roll(table, 64, 1) - table
    leaf_left = -table / (pltpu.roll(table, 127, 1) + 1.0)
    leaf_right = -rest / (pltpu.roll(rest, 127, 1) + 1.0)
    high = jnp.where(codes > 1.5, 1.0, 0.0)
    go_right = jnp.concatenate([codes - 2.0 * high, high], axis=0) > 0.5
    node_here = node[...]
    shift = jnp.zeros((16, 128), F32)
    for n in range(NODES):
        step = jnp.where(
            go_right,
            jnp.broadcast_to(leaf_right[0:1, 2 * n : 2 * n + 1], (16, 128)),
            jnp.broadcast_to(leaf_left[0:1, 2 * n : 2 * n + 1], (16, 128)),
        )
        shift = jnp.where(node_here == n, step, shift)
    moved = margin[...] + shift
    margin_out[...] = moved
    child_out[...] = 2 * node_here + jnp.where(go_right, 1, 0)
    fresh = jax.nn.sigmoid(moved)
    slope = fresh - labels[...]
    curve = fresh * (1.0 - fresh)
    for i in range(16):
        grad_out[0:1, i * 128 : (i + 1) * 128] = slope[i : i + 1, :]
        grad_out[1:2, i * 128 : (i + 1) * 128] = curve[i : i + 1, :]


def rows_update(parts, node, margin, labels, sent):
    return pl.pallas_call(
        rows_kernel,
        out_shape=(
            jax.ShapeDtypeStruct((16, 128), F32),
            jax.ShapeDtypeStruct((16, 128), jnp.int32),
            jax.ShapeDtypeStruct((2, ROWS), F32),
        ),
        in_specs=[VMEM] * 4 + [pl.BlockSpec(memory_space=pl.ANY)],
        out_specs=[VMEM] * 3,
        scratch_shapes=[pltpu.VMEM((8, 128), F32)],
        name="rows_update",
        compiler_params=LIMIT,
        cost_estimate=cost(ROWS * 128, 1 << 17),
    )(parts, node, margin, labels, near(sent))


def share(spread, axes):
    return lax.all_to_all(spread, axes, 0, 0, tiled=True)


def on_device(binned, node_of, margin, labels, split_feature, split_bin):
    swap = [(0, 1), (1, 0)]
    columns = binned.T
    weights, pay = stage(
        far(columns),
        far(node_of.reshape(1, ROWS)),
        far(margin.reshape(1, ROWS)),
        far(labels.reshape(1, ROWS)),
        far(split_feature.reshape(1, NODES)),
        far(split_bin.reshape(1, NODES)),
    )
    line = share(pay, LINE)
    send_a, keep_a = histograms(near(weights), near(columns), 0, CUT)
    arrived_a = lax.ppermute(send_a, "core", swap)
    pay = relay(line, pay)
    parts = share(pay, PLANE)
    own_a, line_a = chip_sum(keep_a, arrived_a, send_a)
    arrived_a = lax.ppermute(line_a, "zl", swap)
    send_b, keep_b = histograms(near(weights), near(columns), CUT, FEATS - CUT)
    arrived_b = lax.ppermute(send_b, "core", swap)
    own_b, line_b = chip_sum(keep_b, arrived_b, send_b)
    arrived_b = lax.ppermute(line_b, "zl", swap)
    histogram = finish(own_a, arrived_a, line_a, 0)
    margin_out, child_out, grad_out = rows_update(
        near(parts),
        near(node_of.reshape(16, 128)),
        near(margin.reshape(16, 128)),
        near(labels.reshape(16, 128)),
        pay,
    )
    histogram = finish(own_b, arrived_b, line_b, CUT, histogram)
    return (
        histogram.reshape(8, 2, FEATS, BINS),
        margin_out.reshape(ROWS),
        child_out.reshape(ROWS),
        grad_out,
    )


def solution(mesh):
    fine = Mesh(mesh.devices.reshape(4, 8, 4, 2, 2), ("x", "y", "zh", "zl", "core"))
    rows = P(ROW_AXES)
    in_specs = (P(ROW_AXES, FEAT_AXES), rows, rows, rows, P(), P())
    out_specs = (P(ROW_AXES, None, FEAT_AXES, None), rows, rows, P(None, ROW_AXES))

    return jax.shard_map(
        on_device, mesh=fine, in_specs=in_specs, out_specs=out_specs, check_vma=False
    )
```

profile of v0, /device:TPU:8, one launch (start us, length us, event | category | flops | bytes accessed | tf_op | source)
XLA Modules:
  0.0 60.5 jit_solution(17609609334143630050)
XLA Ops:
  0.6 0.0 copy-start
  0.6 2.5 %stage.1 = (bf16[64,2048]{1,0:T(8,128)(2,1)S(1)}, f32[16,9,1,128]{3,2,1,0:T(1,128)}) custom-call(s32[64,2048]{1,0:T(8,128)} %bitcast.12, s32[1,2048]{1,0:T(1,128)} %bitcast.15, f32[1,2048]{1,0:T(1,128)} %bitcast.17, f32[1,2048]{1,0:T(1,128)} %bitcast.19, s32[1,32]{1,0:T(1,128)} %bitcast.22, s32[1,32]{1,0:T(1,128)} %bitcast.23), custom_call_target="tpu_custom_call" | custom-call | flops 25165824 | bytes 3145728 | tf_op jit(solution)/shard_map/stage/pallas_call | solution.py:140
  3.1 0.0 copy-done
  3.1 9.1 %shard_map.94 = (bf16[48,32,256]{2,1,0:T(8,128)(2,1)S(1)}, bf16[48,32,256]{2,1,0:T(8,128)(2,1)S(1)}) custom-call(bf16[64,2048]{1,0:T(8,128)(2,1)S(1)} %get-tuple-element.17.weights, s32[64,2048]{1,0:T(8,128)S(1)} %bitcast.13), custom_call_target="tpu_custom_call" | custom-call | flops 3221225472 | bytes 3145728 | tf_op jit(solution)/shard_map/pallas_call | solution.py:175
  12.2 1.9 %collective-permute-start.2 = (bf16[48,32,256]{2,1,0:T(8,128)(2,1)S(1)}, bf16[48,32,256]{2,1,0:T(8,128)(2,1)S(1)}, u32[]{:S(2)}, u32[]{:S(2)}) collective-permute-start(bf16[48,32,256]{2,1,0:T(8,128)(2,1)S(1)} %get-tuple-element.23.sent), channel_id=1, source_target_pairs={{0,1},{1,0},{2,3},{3,2},{4,5},{5,4},{6,7},{7,6},{8,9},{9,8},{10,11... | collective-permute-start | bytes 2359304 | tf_op jit(solution)/shard_map/ppermute | solution.py:328
  14.2 10.6 %all-to-all-start = ((f32[16,9,1,128]{3,2,1,0:T(1,128)}), f32[16,9,1,128]{3,2,1,0:T(1,128)}, u32[]{:S(2)}, u32[]{:S(2)}) async-start(f32[16,9,1,128]{3,2,1,0:T(1,128)} %get-tuple-element.26.sent), calls=%async_computation | async-start | bytes 147456 | tf_op jit(solution)/shard_map/all_to_all | solution.py:312
  24.7 3.7 %shard_map.93 = (bf16[16,32,256]{2,1,0:T(8,128)(2,1)}, bf16[16,32,256]{2,1,0:T(8,128)(2,1)S(1)}) custom-call(bf16[64,2048]{1,0:T(8,128)(2,1)S(1)} %get-tuple-element.17.weights, s32[64,2048]{1,0:T(8,128)S(1)} %bitcast.14), custom_call_target="tpu_custom_call" | custom-call | flops 1073741824 | bytes 3145728 | tf_op jit(solution)/shard_map/pallas_call | solution.py:175
  28.5 0.0 copy-start.1
  28.5 0.7 %copy-done.1 = bf16[16,32,256]{2,1,0:T(8,128)(2,1)} copy-done((bf16[16,32,256]{2,1,0:T(8,128)(2,1)}, bf16[16,32,256]{2,1,0:T(8,128)(2,1)S(1)}, u32[]{:S(2)}) %copy-start.1) | copy-done | bytes 262168
  29.2 2.2 %collective-permute-start = (bf16[16,32,256]{2,1,0:T(8,128)(2,1)}, bf16[16,32,256]{2,1,0:T(8,128)(2,1)}, u32[]{:S(2)}, u32[]{:S(2)}) collective-permute-start(bf16[16,32,256]{2,1,0:T(8,128)(2,1)} %get-tuple-element.19.sent), channel_id=1, source_target_pairs={{0,1},{1,0},{2,3},{3,2},{4,5},{5,4},{6,7},{7,6},{8,9},{9,8},{10,11... | collective-permute-start | bytes 786440 | tf_op jit(solution)/shard_map/ppermute | solution.py:334
  31.4 0.0 collective-permute-done.2.arrived
  31.4 0.2 chip_sum.3
  31.6 0.0 copy-start.2
  31.6 3.7 %collective-permute-start.3 = (bf16[48,16,256]{2,1,0:T(8,128)(2,1)S(1)}, bf16[48,16,256]{2,1,0:T(8,128)(2,1)S(1)}, u32[]{:S(2)}, u32[]{:S(2)}) collective-permute-start(bf16[48,16,256]{2,1,0:T(8,128)(2,1)S(1)} %get-tuple-element.25.sent), channel_id=1, source_target_pairs={{0,2},{2,0},{1,3},{3,1},{4,6},{6,4},{5,7},{7,5},{8,10},{10,8},{9,1... | collective-permute-start | bytes 1179656 | tf_op jit(solution)/shard_map/ppermute | solution.py:332
  35.3 0.0 all-to-all-done.line
  35.3 1.6 %relay.1.sent = f32[32,9,1,128]{3,2,1,0:T(1,128)} custom-call(f32[16,9,1,128]{3,2,1,0:T(1,128)} %all-to-all-done.line, f32[16,9,1,128]{3,2,1,0:T(1,128)} %get-tuple-element.26.sent), custom_call_target="tpu_custom_call" | custom-call | flops 36864 | bytes 131072 | tf_op jit(solution)/shard_map/relay/pallas_call | solution.py:219
  37.0 10.2 %all-to-all-start.1 = ((f32[32,9,1,128]{3,2,1,0:T(1,128)}), f32[32,9,1,128]{3,2,1,0:T(1,128)S(1)}, u32[]{:S(2)}, u32[]{:S(2)}) async-start(f32[32,9,1,128]{3,2,1,0:T(1,128)} %relay.1.sent), calls=%async_computation.1 | async-start | bytes 294912 | tf_op jit(solution)/shard_map/all_to_all | solution.py:312
  47.1 0.0 collective-permute-done.arrived
  47.1 0.0 copy-done.2
  47.1 0.0 copy-start.3
  47.2 0.0 copy-start.4
  47.2 0.0 copy-start.5
  47.2 1.0 %chip_sum.2 = (f32[16,16,256]{2,1,0:T(8,128)S(1)}, bf16[16,16,256]{2,1,0:T(8,128)(2,1)S(1)}) custom-call(bf16[16,32,256]{2,1,0:T(8,128)(2,1)S(1)} %copy-done.2, bf16[16,32,256]{2,1,0:T(8,128)(2,1)} %collective-permute-done.arrived, bf16[16,32,256]{2,1,0:T(8,128)(2,1)} %get-tuple-element.19.sent), custom_call_target="tpu_custom_call" | custom-call | flops 131072 | bytes 3145728 | tf_op jit(solution)/shard_map/chip_sum/pallas_call | solution.py:194
  48.2 2.3 %collective-permute-start.1 = (bf16[16,16,256]{2,1,0:T(8,128)(2,1)S(1)}, bf16[16,16,256]{2,1,0:T(8,128)(2,1)S(1)}, u32[]{:S(2)}, u32[]{:S(2)}) collective-permute-start(bf16[16,16,256]{2,1,0:T(8,128)(2,1)S(1)} %get-tuple-element.21.sent), channel_id=1, source_target_pairs={{0,2},{2,0},{1,3},{3,1},{4,6},{6,4},{5,7},{7,5},{8,10},{10,8},{9,1... | collective-permute-start | bytes 393224 | tf_op jit(solution)/shard_map/ppermute | solution.py:336
  50.5 7.0 %all-to-all-done.1.parts = f32[32,9,1,128]{3,2,1,0:T(1,128)S(1)} async-done(((f32[32,9,1,128]{3,2,1,0:T(1,128)}), f32[32,9,1,128]{3,2,1,0:T(1,128)S(1)}, u32[]{:S(2)}, u32[]{:S(2)}) %all-to-all-start.1) | async-done | bytes 147488 | tf_op jit(solution)/shard_map/all_to_all | solution.py:312
  57.5 0.0 copy-done.3
  57.5 0.0 copy-done.4
  57.5 0.0 copy-done.5
  57.5 1.0 %rows_update.1 = (f32[16,128]{1,0:T(8,128)}, s32[16,128]{1,0:T(8,128)}, f32[2,2048]{1,0:T(2,128)}) custom-call(f32[32,9,1,128]{3,2,1,0:T(1,128)S(1)} %all-to-all-done.1.parts, s32[16,128]{1,0:T(8,128)S(1)} %bitcast.16, f32[16,128]{1,0:T(8,128)S(1)} %bitcast.18, f32[16,128]{1,0:T(8,128)S(1)} %bitcast.20, f32[32,9,1,128]{3,2,1,0:T(1,128)} %relay.1.sent), custom_call_target="tpu_custom_call" | custom-call | flops 262144 | bytes 131072 | tf_op jit(solution)/shard_map/rows_update/pallas_call | solution.py:295
  58.5 0.0 collective-permute-done.3.arrived
  58.5 1.2 %shard_map.95.rest_0_ = f32[16,64,256]{2,1,0:T(8,128)} custom-call(f32[48,16,256]{2,1,0:T(8,128)S(1)} %get-tuple-element.24.own, bf16[48,16,256]{2,1,0:T(8,128)(2,1)S(1)} %collective-permute-done.3.arrived, bf16[48,16,256]{2,1,0:T(8,128)(2,1)S(1)} %get-tuple-element.25.sent), custom_call_target="tpu_custom_call" | custom-call | flops 196608 | bytes 3145728 | tf_op jit(solution)/shard_map/pallas_call | solution.py:245
  59.7 0.0 collective-permute-done.1.arrived
  59.7 0.8 %shard_map.96 = f32[16,64,256]{2,1,0:T(8,128)} custom-call(f32[16,16,256]{2,1,0:T(8,128)S(1)} %get-tuple-element.20.own, bf16[16,16,256]{2,1,0:T(8,128)(2,1)S(1)} %collective-permute-done.1.arrived, bf16[16,16,256]{2,1,0:T(8,128)(2,1)S(1)} %get-tuple-element.21.sent, f32[16,64,256]{2,1,0:T(8,128)} %shard_map.95.rest_0_), custom_call_target="tpu_custom_call", output_to_operand_aliasing={{}: (3, {})} | custom-call | flops 65536 | bytes 3145728 | tf_op jit(solution)/shard_map/pallas_call | solution.py:245
Async XLA Ops:
  0.6 2.5 %copy-start = (s32[2048,64]{0,1:T(8,128)S(1)}, s32[2048,64]{0,1:T(8,128)}, u32[]{:S(2)}) copy-start(s32[2048,64]{0,1:T(8,128)} %param.6) | copy-start | bytes 1572868
  12.2 19.2 %collective-permute-start.2 = (bf16[48,32,256]{2,1,0:T(8,128)(2,1)S(1)}, bf16[48,32,256]{2,1,0:T(8,128)(2,1)S(1)}, u32[]{:S(2)}, u32[]{:S(2)}) collective-permute-start(bf16[48,32,256]{2,1,0:T(8,128)(2,1)S(1)} %get-tuple-element.23.sent), channel_id=1, source_target_pairs={{0,1},{1,0},{2,3},{3,2},{4,5},{5,4},{6,7},{7,6},{8,9},{9,8},{10,11... | collective-permute-start | bytes 2359304 | tf_op jit(solution)/shard_map/ppermute | solution.py:328
  14.2 21.2 %all-to-all-start = ((f32[16,9,1,128]{3,2,1,0:T(1,128)}), f32[16,9,1,128]{3,2,1,0:T(1,128)}, u32[]{:S(2)}, u32[]{:S(2)}) async-start(f32[16,9,1,128]{3,2,1,0:T(1,128)} %get-tuple-element.26.sent), calls=%async_computation | async-start | bytes 147456 | tf_op jit(solution)/shard_map/all_to_all | solution.py:312
  28.5 0.7 %copy-start.1 = (bf16[16,32,256]{2,1,0:T(8,128)(2,1)}, bf16[16,32,256]{2,1,0:T(8,128)(2,1)S(1)}, u32[]{:S(2)}) copy-start(bf16[16,32,256]{2,1,0:T(8,128)(2,1)S(1)} %get-tuple-element.18.keep) | copy-start | bytes 786436
  29.2 18.0 %collective-permute-start = (bf16[16,32,256]{2,1,0:T(8,128)(2,1)}, bf16[16,32,256]{2,1,0:T(8,128)(2,1)}, u32[]{:S(2)}, u32[]{:S(2)}) collective-permute-start(bf16[16,32,256]{2,1,0:T(8,128)(2,1)} %get-tuple-element.19.sent), channel_id=1, source_target_pairs={{0,1},{1,0},{2,3},{3,2},{4,5},{5,4},{6,7},{7,6},{8,9},{9,8},{10,11... | collective-permute-start | bytes 786440 | tf_op jit(solution)/shard_map/ppermute | solution.py:334
  31.6 15.5 %copy-start.2 = (bf16[16,32,256]{2,1,0:T(8,128)(2,1)S(1)}, bf16[16,32,256]{2,1,0:T(8,128)(2,1)}, u32[]{:S(2)}) copy-start(bf16[16,32,256]{2,1,0:T(8,128)(2,1)} %copy-done.1) | copy-start | bytes 786436
  31.6 26.9 %collective-permute-start.3 = (bf16[48,16,256]{2,1,0:T(8,128)(2,1)S(1)}, bf16[48,16,256]{2,1,0:T(8,128)(2,1)S(1)}, u32[]{:S(2)}, u32[]{:S(2)}) collective-permute-start(bf16[48,16,256]{2,1,0:T(8,128)(2,1)S(1)} %get-tuple-element.25.sent), channel_id=1, source_target_pairs={{0,2},{2,0},{1,3},{3,1},{4,6},{6,4},{5,7},{7,5},{8,10},{10,8},{9,1... | collective-permute-start | bytes 1179656 | tf_op jit(solution)/shard_map/ppermute | solution.py:332
  37.0 20.6 %all-to-all-start.1 = ((f32[32,9,1,128]{3,2,1,0:T(1,128)}), f32[32,9,1,128]{3,2,1,0:T(1,128)S(1)}, u32[]{:S(2)}, u32[]{:S(2)}) async-start(f32[32,9,1,128]{3,2,1,0:T(1,128)} %relay.1.sent), calls=%async_computation.1 | async-start | bytes 294912 | tf_op jit(solution)/shard_map/all_to_all | solution.py:312
  47.1 10.4 %copy-start.3 = (s32[2048]{0:T(1024)S(1)}, s32[2048]{0:T(1024)}, u32[]{:S(2)}) copy-start(s32[2048]{0:T(1024)} %param.7) | copy-start | bytes 24580
  47.2 10.4 %copy-start.4 = (f32[2048]{0:T(1024)S(1)}, f32[2048]{0:T(1024)}, u32[]{:S(2)}) copy-start(f32[2048]{0:T(1024)} %param.8) | copy-start | bytes 24580
  47.2 10.4 %copy-start.5 = (f32[2048]{0:T(1024)S(1)}, f32[2048]{0:T(1024)}, u32[]{:S(2)}) copy-start(f32[2048]{0:T(1024)} %param.9) | copy-start | bytes 24580
  48.2 11.5 %collective-permute-start.1 = (bf16[16,16,256]{2,1,0:T(8,128)(2,1)S(1)}, bf16[16,16,256]{2,1,0:T(8,128)(2,1)S(1)}, u32[]{:S(2)}, u32[]{:S(2)}) collective-permute-start(bf16[16,16,256]{2,1,0:T(8,128)(2,1)S(1)} %get-tuple-element.21.sent), channel_id=1, source_target_pairs={{0,2},{2,0},{1,3},{3,1},{4,6},{6,4},{5,7},{7,5},{8,10},{10,8},{9,1... | collective-permute-start | bytes 393224 | tf_op jit(solution)/shard_map/ppermute | solution.py:336
where the time goes:
time: 61 us; the launch traced here: 60.5 us
  starting transfers between devices  30.9 us (51%)
  Pallas kernels  21.1 us (35%)
  waiting for transfers between devices  7.03 us (12%)
  between operations  0.77 us (1%)
  local copies, waits for them, and re-layouts  0.72 us (1%)
    all_to_all x2, starting transfers between devices, share(): return lax.all_to_all(spread, axes, 0, 0, tiled=True)  20.7 us
    pallas_call x2, Pallas kernels, histograms(): pl.pallas_call(functools.partial(histogram_kernel, first, count), out_sha...  12.8 us
    all_to_all x2, waiting for transfers between devices, share(): return lax.all_to_all(spread, axes, 0, 0, tiled=True)  7.02 us
    ppermute x1, starting transfers between devices, on_device(): arrived_a = lax.ppermute(line_a, 'zl', swap)  3.68 us
    pallas_call x1, Pallas kernels, stage(): pl.pallas_call(stage_kernel, out_shape=(pltpu.VMEM((2 * NODES, ROWS), BF1...  2.48 us
    ppermute x1, starting transfers between devices, on_device(): arrived_b = lax.ppermute(line_b, 'zl', swap)  2.29 us
    ppermute x1, starting transfers between devices, on_device(): arrived_b = lax.ppermute(send_b, 'core', swap)  2.25 us
    pallas_call x2, Pallas kernels, finish(): pl.pallas_call(functools.partial(finish_kernel, count), out_shape=jax.Sha...  2 us
  transfers between devices with their start and end apart: 6, of which 1 were waited for; matrix products, arithmetic and copies ran while one was open for 0% of the time, Pallas kernels for 14%

commit v1 on v0

--- a/solution.py
+++ b/solution.py
@@ -59,29 +59,6 @@
         piece = contract_last(jnp.concatenate(split, axis=0), hot)
         total = piece if total is None else total + piece
     return total
-
-
-def pair_sums(weights, row_of, row_of_next):
-    low_ids = iota((BINS // 2, TILE), 0).astype(I16)
-    one, zero = BF16(1), BF16(0)
-    total = None
-    for k in range(ROWS // TILE):
-        tile = weights[:, k * TILE : (k + 1) * TILE]
-        parts, hots = [tile], []
-        for source in (row_of, row_of_next):
-            row = jnp.broadcast_to(source(k), (16, TILE))
-            low = jnp.concatenate([(row & 127).astype(I16)] * 8, axis=0)
-            high = jnp.concatenate([(row >> 7).astype(I16)] * 4, axis=0)
-            parts.append(jnp.where(high == 1, tile, zero))
-            hots.append(jnp.where(low_ids == low, one, zero))
-        piece = contract_last(jnp.concatenate(parts, axis=0), jnp.concatenate(hots, axis=0))
-        total = piece if total is None else total + piece
-    sums = []
-    for i in range(2):
-        span = slice(i * 128, (i + 1) * 128)
-        upper = total[64 * (i + 1) : 64 * (i + 2), span]
-        sums.append((total[:64, span] - upper, upper))
-    return sums
 
 
 def stage_kernel(columns, node, margin, labels, feature, cut, weights, pay, chosen):
@@ -153,21 +130,17 @@
 
 
 def histogram_kernel(first, count, weights, columns, send, keep):
-    def pair(p, carry):
-        f = 2 * p
-
-        def source(g):
-            return lambda k: columns[pl.ds(first + g, 1), k * TILE : (k + 1) * TILE]
-
-        for i, halves in enumerate(pair_sums(weights, source(f), source(f + 1))):
-            for h in range(2):
-                span = slice(h * 128, (h + 1) * 128)
-                sums = halves[h].astype(BF16)
-                send[f + i, :, span] = sums[:NODES]
-                keep[f + i, :, span] = sums[NODES:]
+    def feature(f, carry):
+        sums = bin_sums(
+            weights, lambda k: columns[pl.ds(first + f, 1), k * TILE : (k + 1) * TILE]
+        ).astype(BF16)
+        for h in range(2):
+            span = slice(h * 128, (h + 1) * 128)
+            send[f, :, span] = sums[64 * h : 64 * h + NODES]
+            keep[f, :, span] = sums[64 * h + NODES : 64 * h + 64]
         return carry
 
-    lax.fori_loop(0, count // 2, pair, 0, unroll=4)
+    lax.fori_loop(0, count, feature, 0, unroll=count)
 
 
 def histograms(weights, columns, first, count):

time: 61 us -> 57.8 us (0.948)
  Pallas kernels: 21.1 us -> 18 us
    pallas_call x2, Pallas kernels: 12.8 us -> 9.7 us  [histograms(): pl.pallas_call(functools.partial(histogram_kernel, first, count), out_sha...]
where the time goes in v1:
time: 57.8 us; the launch traced here: 57.4 us
  starting transfers between devices  30.9 us (53%)
  Pallas kernels  18 us (31%)
  waiting for transfers between devices  7.02 us (12%)
  between operations  0.78 us (1%)
  local copies, waits for them, and re-layouts  0.72 us (1%)
    all_to_all x2, starting transfers between devices, share(): return lax.all_to_all(spread, axes, 0, 0, tiled=True)  20.7 us
    pallas_call x2, Pallas kernels, histograms(): pl.pallas_call(functools.partial(histogram_kernel, first, count), out_sha...  9.7 us
    all_to_all x2, waiting for transfers between devices, share(): return lax.all_to_all(spread, axes, 0, 0, tiled=True)  7.01 us
    ppermute x1, starting transfers between devices, on_device(): arrived_a = lax.ppermute(line_a, 'zl', swap)  3.67 us
    pallas_call x1, Pallas kernels, stage(): pl.pallas_call(stage_kernel, out_shape=(pltpu.VMEM((2 * NODES, ROWS), BF1...  2.48 us
    ppermute x1, starting transfers between devices, on_device(): arrived_b = lax.ppermute(line_b, 'zl', swap)  2.3 us
    ppermute x1, starting transfers between devices, on_device(): arrived_b = lax.ppermute(send_b, 'core', swap)  2.26 us
    pallas_call x2, Pallas kernels, finish(): pl.pallas_call(functools.partial(finish_kernel, count), out_shape=jax.Sha...  2 us
  transfers between devices with their start and end apart: 6, of which 1 were waited for; matrix products, arithmetic and copies ran while one was open for 0% of the time, Pallas kernels for 14%

profile of v1, /device:TPU:8, one launch (start us, length us, event | category | flops | bytes accessed | tf_op | source)
XLA Modules:
  0.0 57.4 jit_solution(11369269911613247088)
XLA Ops:
  0.6 0.0 copy-start
  0.6 2.5 %stage.1 = (bf16[64,2048]{1,0:T(8,128)(2,1)S(1)}, f32[16,9,1,128]{3,2,1,0:T(1,128)}) custom-call(s32[64,2048]{1,0:T(8,128)} %bitcast.12, s32[1,2048]{1,0:T(1,128)} %bitcast.15, f32[1,2048]{1,0:T(1,128)} %bitcast.17, f32[1,2048]{1,0:T(1,128)} %bitcast.19, s32[1,32]{1,0:T(1,128)} %bitcast.22, s32[1,32]{1,0:T(1,128)} %bitcast.23), custom_call_target="tpu_custom_call" | custom-call | flops 25165824 | bytes 3145728 | tf_op jit(solution)/shard_map/stage/pallas_call | solution.py:117
  3.1 0.0 copy-done
  3.1 6.7 %shard_map.94 = (bf16[48,32,256]{2,1,0:T(8,128)(2,1)S(1)}, bf16[48,32,256]{2,1,0:T(8,128)(2,1)S(1)}) custom-call(bf16[64,2048]{1,0:T(8,128)(2,1)S(1)} %get-tuple-element.17.weights, s32[64,2048]{1,0:T(8,128)S(1)} %bitcast.13), custom_call_target="tpu_custom_call" | custom-call | flops 3221225472 | bytes 3145728 | tf_op jit(solution)/shard_map/pallas_call | solution.py:148
  9.8 1.9 %collective-permute-start.2 = (bf16[48,32,256]{2,1,0:T(8,128)(2,1)S(1)}, bf16[48,32,256]{2,1,0:T(8,128)(2,1)S(1)}, u32[]{:S(2)}, u32[]{:S(2)}) collective-permute-start(bf16[48,32,256]{2,1,0:T(8,128)(2,1)S(1)} %get-tuple-element.23.sent), channel_id=1, source_target_pairs={{0,1},{1,0},{2,3},{3,2},{4,5},{5,4},{6,7},{7,6},{8,9},{9,8},{10,11... | collective-permute-start | bytes 2359304 | tf_op jit(solution)/shard_map/ppermute | solution.py:301
  11.7 10.6 %all-to-all-start = ((f32[16,9,1,128]{3,2,1,0:T(1,128)}), f32[16,9,1,128]{3,2,1,0:T(1,128)}, u32[]{:S(2)}, u32[]{:S(2)}) async-start(f32[16,9,1,128]{3,2,1,0:T(1,128)} %get-tuple-element.26.sent), calls=%async_computation | async-start | bytes 147456 | tf_op jit(solution)/shard_map/all_to_all | solution.py:285
  22.3 3.0 %shard_map.93 = (bf16[16,32,256]{2,1,0:T(8,128)(2,1)}, bf16[16,32,256]{2,1,0:T(8,128)(2,1)S(1)}) custom-call(bf16[64,2048]{1,0:T(8,128)(2,1)S(1)} %get-tuple-element.17.weights, s32[64,2048]{1,0:T(8,128)S(1)} %bitcast.14), custom_call_target="tpu_custom_call" | custom-call | flops 1073741824 | bytes 3145728 | tf_op jit(solution)/shard_map/pallas_call | solution.py:148
  25.3 0.0 copy-start.1
  25.3 0.7 %copy-done.1 = bf16[16,32,256]{2,1,0:T(8,128)(2,1)} copy-done((bf16[16,32,256]{2,1,0:T(8,128)(2,1)}, bf16[16,32,256]{2,1,0:T(8,128)(2,1)S(1)}, u32[]{:S(2)}) %copy-start.1) | copy-done | bytes 262168
  26.0 2.3 %collective-permute-start = (bf16[16,32,256]{2,1,0:T(8,128)(2,1)}, bf16[16,32,256]{2,1,0:T(8,128)(2,1)}, u32[]{:S(2)}, u32[]{:S(2)}) collective-permute-start(bf16[16,32,256]{2,1,0:T(8,128)(2,1)} %get-tuple-element.19.sent), channel_id=1, source_target_pairs={{0,1},{1,0},{2,3},{3,2},{4,5},{5,4},{6,7},{7,6},{8,9},{9,8},{10,11... | collective-permute-start | bytes 786440 | tf_op jit(solution)/shard_map/ppermute | solution.py:307
  28.3 0.0 collective-permute-done.2.arrived
  28.3 0.2 chip_sum.3
  28.5 0.0 copy-start.2
  28.5 3.7 %collective-permute-start.3 = (bf16[48,16,256]{2,1,0:T(8,128)(2,1)S(1)}, bf16[48,16,256]{2,1,0:T(8,128)(2,1)S(1)}, u32[]{:S(2)}, u32[]{:S(2)}) collective-permute-start(bf16[48,16,256]{2,1,0:T(8,128)(2,1)S(1)} %get-tuple-element.25.sent), channel_id=1, source_target_pairs={{0,2},{2,0},{1,3},{3,1},{4,6},{6,4},{5,7},{7,5},{8,10},{10,8},{9,1... | collective-permute-start | bytes 1179656 | tf_op jit(solution)/shard_map/ppermute | solution.py:305
  32.2 0.0 all-to-all-done.line
  32.2 1.6 %relay.1.sent = f32[32,9,1,128]{3,2,1,0:T(1,128)} custom-call(f32[16,9,1,128]{3,2,1,0:T(1,128)} %all-to-all-done.line, f32[16,9,1,128]{3,2,1,0:T(1,128)} %get-tuple-element.26.sent), custom_call_target="tpu_custom_call" | custom-call | flops 36864 | bytes 131072 | tf_op jit(solution)/shard_map/relay/pallas_call | solution.py:192
  33.8 10.2 %all-to-all-start.1 = ((f32[32,9,1,128]{3,2,1,0:T(1,128)}), f32[32,9,1,128]{3,2,1,0:T(1,128)S(1)}, u32[]{:S(2)}, u32[]{:S(2)}) async-start(f32[32,9,1,128]{3,2,1,0:T(1,128)} %relay.1.sent), calls=%async_computation.1 | async-start | bytes 294912 | tf_op jit(solution)/shard_map/all_to_all | solution.py:285
  44.0 0.0 collective-permute-done.arrived
  44.0 0.0 copy-done.2
  44.0 0.0 copy-start.3
  44.0 0.0 copy-start.4
  44.0 0.0 copy-start.5
  44.0 1.0 %chip_sum.2 = (f32[16,16,256]{2,1,0:T(8,128)S(1)}, bf16[16,16,256]{2,1,0:T(8,128)(2,1)S(1)}) custom-call(bf16[16,32,256]{2,1,0:T(8,128)(2,1)S(1)} %copy-done.2, bf16[16,32,256]{2,1,0:T(8,128)(2,1)} %collective-permute-done.arrived, bf16[16,32,256]{2,1,0:T(8,128)(2,1)} %get-tuple-element.19.sent), custom_call_target="tpu_custom_call" | custom-call | flops 131072 | bytes 3145728 | tf_op jit(solution)/shard_map/chip_sum/pallas_call | solution.py:167
  45.1 2.3 %collective-permute-start.1 = (bf16[16,16,256]{2,1,0:T(8,128)(2,1)S(1)}, bf16[16,16,256]{2,1,0:T(8,128)(2,1)S(1)}, u32[]{:S(2)}, u32[]{:S(2)}) collective-permute-start(bf16[16,16,256]{2,1,0:T(8,128)(2,1)S(1)} %get-tuple-element.21.sent), channel_id=1, source_target_pairs={{0,2},{2,0},{1,3},{3,1},{4,6},{6,4},{5,7},{7,5},{8,10},{10,8},{9,1... | collective-permute-start | bytes 393224 | tf_op jit(solution)/shard_map/ppermute | solution.py:309
  47.4 7.0 %all-to-all-done.1.parts = f32[32,9,1,128]{3,2,1,0:T(1,128)S(1)} async-done(((f32[32,9,1,128]{3,2,1,0:T(1,128)}), f32[32,9,1,128]{3,2,1,0:T(1,128)S(1)}, u32[]{:S(2)}, u32[]{:S(2)}) %all-to-all-start.1) | async-done | bytes 147488 | tf_op jit(solution)/shard_map/all_to_all | solution.py:285
  54.4 0.0 copy-done.3
  54.4 0.0 copy-done.4
  54.4 0.0 copy-done.5
  54.4 1.0 %rows_update.1 = (f32[16,128]{1,0:T(8,128)}, s32[16,128]{1,0:T(8,128)}, f32[2,2048]{1,0:T(2,128)}) custom-call(f32[32,9,1,128]{3,2,1,0:T(1,128)S(1)} %all-to-all-done.1.parts, s32[16,128]{1,0:T(8,128)S(1)} %bitcast.16, f32[16,128]{1,0:T(8,128)S(1)} %bitcast.18, f32[16,128]{1,0:T(8,128)S(1)} %bitcast.20, f32[32,9,1,128]{3,2,1,0:T(1,128)} %relay.1.sent), custom_call_target="tpu_custom_call" | custom-call | flops 262144 | bytes 131072 | tf_op jit(solution)/shard_map/rows_update/pallas_call | solution.py:268
  55.4 0.0 collective-permute-done.3.arrived
  55.4 1.2 %shard_map.95.rest_0_ = f32[16,64,256]{2,1,0:T(8,128)} custom-call(f32[48,16,256]{2,1,0:T(8,128)S(1)} %get-tuple-element.24.own, bf16[48,16,256]{2,1,0:T(8,128)(2,1)S(1)} %collective-permute-done.3.arrived, bf16[48,16,256]{2,1,0:T(8,128)(2,1)S(1)} %get-tuple-element.25.sent), custom_call_target="tpu_custom_call" | custom-call | flops 196608 | bytes 3145728 | tf_op jit(solution)/shard_map/pallas_call | solution.py:218
  56.6 0.0 collective-permute-done.1.arrived
  56.6 0.8 %shard_map.96 = f32[16,64,256]{2,1,0:T(8,128)} custom-call(f32[16,16,256]{2,1,0:T(8,128)S(1)} %get-tuple-element.20.own, bf16[16,16,256]{2,1,0:T(8,128)(2,1)S(1)} %collective-permute-done.1.arrived, bf16[16,16,256]{2,1,0:T(8,128)(2,1)S(1)} %get-tuple-element.21.sent, f32[16,64,256]{2,1,0:T(8,128)} %shard_map.95.rest_0_), custom_call_target="tpu_custom_call", output_to_operand_aliasing={{}: (3, {})} | custom-call | flops 65536 | bytes 3145728 | tf_op jit(solution)/shard_map/pallas_call | solution.py:218
Async XLA Ops:
  0.6 2.5 %copy-start = (s32[2048,64]{0,1:T(8,128)S(1)}, s32[2048,64]{0,1:T(8,128)}, u32[]{:S(2)}) copy-start(s32[2048,64]{0,1:T(8,128)} %param.6) | copy-start | bytes 1572868
  9.8 18.5 %collective-permute-start.2 = (bf16[48,32,256]{2,1,0:T(8,128)(2,1)S(1)}, bf16[48,32,256]{2,1,0:T(8,128)(2,1)S(1)}, u32[]{:S(2)}, u32[]{:S(2)}) collective-permute-start(bf16[48,32,256]{2,1,0:T(8,128)(2,1)S(1)} %get-tuple-element.23.sent), channel_id=1, source_target_pairs={{0,1},{1,0},{2,3},{3,2},{4,5},{5,4},{6,7},{7,6},{8,9},{9,8},{10,11... | collective-permute-start | bytes 2359304 | tf_op jit(solution)/shard_map/ppermute | solution.py:301
  11.7 20.5 %all-to-all-start = ((f32[16,9,1,128]{3,2,1,0:T(1,128)}), f32[16,9,1,128]{3,2,1,0:T(1,128)}, u32[]{:S(2)}, u32[]{:S(2)}) async-start(f32[16,9,1,128]{3,2,1,0:T(1,128)} %get-tuple-element.26.sent), calls=%async_computation | async-start | bytes 147456 | tf_op jit(solution)/shard_map/all_to_all | solution.py:285
  25.3 0.7 %copy-start.1 = (bf16[16,32,256]{2,1,0:T(8,128)(2,1)}, bf16[16,32,256]{2,1,0:T(8,128)(2,1)S(1)}, u32[]{:S(2)}) copy-start(bf16[16,32,256]{2,1,0:T(8,128)(2,1)S(1)} %get-tuple-element.18.keep) | copy-start | bytes 786436
  26.0 18.0 %collective-permute-start = (bf16[16,32,256]{2,1,0:T(8,128)(2,1)}, bf16[16,32,256]{2,1,0:T(8,128)(2,1)}, u32[]{:S(2)}, u32[]{:S(2)}) collective-permute-start(bf16[16,32,256]{2,1,0:T(8,128)(2,1)} %get-tuple-element.19.sent), channel_id=1, source_target_pairs={{0,1},{1,0},{2,3},{3,2},{4,5},{5,4},{6,7},{7,6},{8,9},{9,8},{10,11... | collective-permute-start | bytes 786440 | tf_op jit(solution)/shard_map/ppermute | solution.py:307
  28.5 15.5 %copy-start.2 = (bf16[16,32,256]{2,1,0:T(8,128)(2,1)S(1)}, bf16[16,32,256]{2,1,0:T(8,128)(2,1)}, u32[]{:S(2)}) copy-start(bf16[16,32,256]{2,1,0:T(8,128)(2,1)} %copy-done.1) | copy-start | bytes 786436
  28.5 26.9 %collective-permute-start.3 = (bf16[48,16,256]{2,1,0:T(8,128)(2,1)S(1)}, bf16[48,16,256]{2,1,0:T(8,128)(2,1)S(1)}, u32[]{:S(2)}, u32[]{:S(2)}) collective-permute-start(bf16[48,16,256]{2,1,0:T(8,128)(2,1)S(1)} %get-tuple-element.25.sent), channel_id=1, source_target_pairs={{0,2},{2,0},{1,3},{3,1},{4,6},{6,4},{5,7},{7,5},{8,10},{10,8},{9,1... | collective-permute-start | bytes 1179656 | tf_op jit(solution)/shard_map/ppermute | solution.py:305
  33.8 20.6 %all-to-all-start.1 = ((f32[32,9,1,128]{3,2,1,0:T(1,128)}), f32[32,9,1,128]{3,2,1,0:T(1,128)S(1)}, u32[]{:S(2)}, u32[]{:S(2)}) async-start(f32[32,9,1,128]{3,2,1,0:T(1,128)} %relay.1.sent), calls=%async_computation.1 | async-start | bytes 294912 | tf_op jit(solution)/shard_map/all_to_all | solution.py:285
  44.0 10.4 %copy-start.3 = (s32[2048]{0:T(1024)S(1)}, s32[2048]{0:T(1024)}, u32[]{:S(2)}) copy-start(s32[2048]{0:T(1024)} %param.7) | copy-start | bytes 24580
  44.0 10.4 %copy-start.4 = (f32[2048]{0:T(1024)S(1)}, f32[2048]{0:T(1024)}, u32[]{:S(2)}) copy-start(f32[2048]{0:T(1024)} %param.8) | copy-start | bytes 24580
  44.0 10.4 %copy-start.5 = (f32[2048]{0:T(1024)S(1)}, f32[2048]{0:T(1024)}, u32[]{:S(2)}) copy-start(f32[2048]{0:T(1024)} %param.9) | copy-start | bytes 24580
  45.1 11.5 %collective-permute-start.1 = (bf16[16,16,256]{2,1,0:T(8,128)(2,1)S(1)}, bf16[16,16,256]{2,1,0:T(8,128)(2,1)S(1)}, u32[]{:S(2)}, u32[]{:S(2)}) collective-permute-start(bf16[16,16,256]{2,1,0:T(8,128)(2,1)S(1)} %get-tuple-element.21.sent), channel_id=1, source_target_pairs={{0,2},{2,0},{1,3},{3,1},{4,6},{6,4},{5,7},{7,5},{8,10},{10,8},{9,1... | collective-permute-start | bytes 393224 | tf_op jit(solution)/shard_map/ppermute | solution.py:309
